TPU v7x, 128 devices: a whole 4x4x4 slice. The times are simulated.
128 devices in a mesh: batch: 4 (over y), seq: 32 (over z, x, core).
Axes of the slice: x: 4, y: 4, z: 4, core: 2. Of those that a mesh axis runs over, the one named last changes fastest.
Arguments:
- queries: bfloat16 [4, 8192, 1024], P('batch', 'seq'), may hold values from -6 to 6
- key_states: bfloat16 [4, 8192, 1024], P('batch', 'seq'), may hold values from -6 to 6
- value_states: bfloat16 [4, 8192, 1024], P('batch', 'seq'), may hold values from -6 to 6
- out_grad: bfloat16 [4, 8192, 1024], P('batch', 'seq'), may hold values from -6 to 6
- memory: float32 [1024, 1024], replicated, may hold values from -6 to 6
- near_device: int32 [64, 8], replicated, may hold values from 0 to 31, all different within a row; in each aligned block of 2 rows (0 to 1, 2 to 3, ...) no two rows name the same one
- near_slot: int32 [64, 8], replicated, may hold values from 0 to 1
- near_count: int32 [64], replicated, may hold values from 1 to 8, 288 in all
- writer_block: int32 [1024], replicated, may hold values from 0 to 63, as said below
Outputs:
- attended: bfloat16 [4, 8192, 1024], P('batch', 'seq')
- query_grad: bfloat16 [4, 8192, 1024], P('batch', 'seq')
- key_grad: bfloat16 [4, 8192, 1024], P('batch', 'seq')
- value_grad: bfloat16 [4, 8192, 1024], P('batch', 'seq')
- memory_grad: float32 [1024, 1024], P('seq')
Inputs may be any that keep to these rules, and one draw needn't show every extreme that they name: Row n of near_device belongs to block n; one row names different indices; the rows of the 2 blocks of one index of seq name no index more than 1 times. writer_block[r] // 2 == r // 32: a memory row is written by a block of the index of seq that holds the row.
All inputs are finite; a program needn't handle non-finite values.
Results may differ from a plain program's by a relative error of at most 0.025.
Values may be sent and summed in bfloat16 or wider, within the bound.
No kernel may reach another device: no remote copies, remote signals or barrier semaphores. Data moves between devices by JAX's collectives and lax.ppermute only.
A program may use at most 192 MiB of HBM per device.

v0:
```python
import math

import jax
import jax.numpy as jnp
from jax import lax
from jax.experimental import pallas as pl
from jax.experimental.pallas import tpu as pltpu
from jax.sharding import PartitionSpec as P

HEADS = 8
HD = 128
BLK = 128
MEM = 1024
NEAR = 8


def _rows_of(col):
    eye = lax.broadcasted_iota(jnp.int32, (BLK, BLK), 0) == lax.broadcasted_iota(jnp.int32, (BLK, BLK), 1)
    return jnp.sum(jnp.where(eye, col, 0.0), axis=0, keepdims=True)


def _query_body(cnt_ref, nb_ref, q_ref, do_ref, mk_ref, *rest):
    k_refs = rest[:NEAR]
    v_refs = rest[NEAR : 2 * NEAR]
    o_ref, dq_ref, tm_ref, st_ref = rest[2 * NEAR :]
    n = pl.program_id(0)
    h = pl.program_id(1)
    heads = pl.num_programs(1)
    scale = 1.0 / math.sqrt(HD)
    f32 = jnp.float32
    nt = (((1,), (1,)), ((), ()))
    tn = (((0,), (0,)), ((), ()))
    q = q_ref[...]
    do = do_ref[...]
    mk = mk_ref[...]
    nk = jnp.concatenate([r[...] for r in k_refs], axis=0)
    nv = jnp.concatenate([r[...] for r in v_refs], axis=0)
    sm = lax.dot_general(q, mk, nt, preferred_element_type=f32) * scale
    sn = lax.dot_general(q, nk, nt, preferred_element_type=f32) * scale
    col = lax.broadcasted_iota(jnp.int32, sn.shape, 1) // BLK
    sn = jnp.where(col < cnt_ref[n], sn, -jnp.inf)
    m = jnp.maximum(jnp.max(sm, axis=1, keepdims=True), jnp.max(sn, axis=1, keepdims=True))
    em = jnp.exp(sm - m)
    en = jnp.exp(sn - m)
    total = jnp.sum(em, axis=1, keepdims=True) + jnp.sum(en, axis=1, keepdims=True)
    pm = em / total
    pn = en / total
    wm = pm.astype(jnp.bfloat16)
    wn = pn.astype(jnp.bfloat16)
    o = (
        jnp.dot(wm, mk, preferred_element_type=f32) + jnp.dot(wn, nv, preferred_element_type=f32)
    ).astype(jnp.bfloat16)
    o_ref[...] = o
    gd = jnp.sum(do.astype(f32) * o.astype(f32), axis=1, keepdims=True)
    dpm = lax.dot_general(do, mk, nt, preferred_element_type=f32)
    dpn = lax.dot_general(do, nv, nt, preferred_element_type=f32)
    dsm = (pm * (dpm - gd)).astype(jnp.bfloat16)
    dsn = (pn * (dpn - gd)).astype(jnp.bfloat16)
    dq_ref[...] = (
        (jnp.dot(dsm, mk, preferred_element_type=f32) + jnp.dot(dsn, nk, preferred_element_type=f32))
        * scale
    ).astype(jnp.bfloat16)
    tm_ref[0] = lax.dot_general(dsm, q, tn, preferred_element_type=f32) * scale + lax.dot_general(
        wm, do, tn, preferred_element_type=f32
    )
    st_ref[pl.ds(h, 1), :] = _rows_of(m)
    st_ref[pl.ds(heads + h, 1), :] = _rows_of(total)
    st_ref[pl.ds(2 * heads + h, 1), :] = _rows_of(gd)


def query_core(counts, near_rows, q, do, mk, kv_all):
    tokens, width = q.shape
    blocks = tokens // BLK
    mem = mk.shape[0]
    heads = width // HD
    nrows = NEAR * BLK
    qspec = pl.BlockSpec((BLK, HD), lambda n, h, c, t: (n, h))
    mspec = pl.BlockSpec((mem, HD), lambda n, h, c, t: (0, h))

    def kv_spec(j, which):
        return pl.BlockSpec((BLK, HD), lambda n, h, c, t: (t[n * NEAR + j], which * heads + h))

    flops = 2 * tokens * width * (mem + nrows) * 4 + 2 * tokens * width * (nrows + mem * 2)
    grid_spec = pltpu.PrefetchScalarGridSpec(
        num_scalar_prefetch=2,
        grid=(blocks, heads),
        in_specs=[qspec, qspec, mspec]
        + [kv_spec(j, 0) for j in range(NEAR)]
        + [kv_spec(j, 1) for j in range(NEAR)],
        out_specs=[
            qspec,
            qspec,
            pl.BlockSpec((1, mem, HD), lambda n, h, c, t: (n, 0, h)),
            pl.BlockSpec((3 * heads, BLK), lambda n, h, c, t: (0, n)),
        ],
    )
    return pl.pallas_call(
        _query_body,
        grid_spec=grid_spec,
        out_shape=[
            jax.ShapeDtypeStruct((tokens, width), jnp.bfloat16),
            jax.ShapeDtypeStruct((tokens, width), jnp.bfloat16),
            jax.ShapeDtypeStruct((blocks, mem, width), jnp.float32),
            jax.ShapeDtypeStruct((3 * heads, tokens), jnp.float32),
        ],
        compiler_params=pltpu.CompilerParams(dimension_semantics=("arbitrary", "arbitrary")),
        cost_estimate=pl.CostEstimate(
            flops=flops,
            transcendentals=tokens * heads * (mem + nrows),
            bytes_accessed=2 * (4 * tokens * width + blocks * mem * width + 2 * blocks * nrows * width)
            + 4 * blocks * mem * width,
        ),
    )(counts, near_rows, q, do, mk, *([kv_all] * (2 * NEAR)))


def _owner_body(
    src_blk, src_dev, src_slot, src_live, my_slot, qd_ref, st_ref, k_ref, v_ref, sp_ref, dk_out, dv_out, dk_ref, dv_ref
):
    s = pl.program_id(0)
    heads = k_ref.shape[1] // HD
    scale = 1.0 / math.sqrt(HD)
    f32 = jnp.float32
    nt = (((1,), (1,)), ((), ()))

    @pl.when(s == 0)
    def _():
        dk_ref[...] = jnp.zeros(dk_ref.shape, f32)
        dv_ref[...] = jnp.zeros(dv_ref.shape, f32)

    @pl.when(src_live[s] != 0)
    def _():
        rows = pl.ds(pl.multiple_of(my_slot[s] * BLK, BLK), BLK)
        st = st_ref[0]
        for h in range(heads):
            cols = pl.ds(h * HD, HD)
            q_h = qd_ref[:, cols]
            do_h = qd_ref[:, pl.ds((heads + h) * HD, HD)]
            k_h = k_ref[rows, cols]
            v_h = v_ref[rows, cols]
            row_max = st[h : h + 1]
            row_total = st[heads + h : heads + h + 1]
            grad_dot = st[2 * heads + h : 2 * heads + h + 1]
            score_t = lax.dot_general(k_h, q_h, nt, preferred_element_type=f32) * scale
            prob_t = jnp.exp(score_t - row_max) / row_total
            weight_t = prob_t.astype(jnp.bfloat16)
            dprob_t = lax.dot_general(v_h, do_h, nt, preferred_element_type=f32)
            dscore_t = (prob_t * (dprob_t - grad_dot)).astype(jnp.bfloat16)
            dk = (jnp.dot(dscore_t, q_h, preferred_element_type=f32) * scale).astype(jnp.bfloat16)
            dv = jnp.dot(weight_t, do_h, preferred_element_type=f32).astype(jnp.bfloat16)
            dk_ref[rows, cols] += dk.astype(f32)
            dv_ref[rows, cols] += dv.astype(f32)

    @pl.when(s == pl.num_programs(0) - 1)
    def _():
        dk_out[...] = dk_ref[...].astype(dk_out.dtype)
        for l in range(dk_ref.shape[0] // BLK):
            block_rows = slice(l * BLK, (l + 1) * BLK)
            dv_out[block_rows, :] = (dv_ref[block_rows, :] + sp_ref[l : l + 1, :]).astype(dv_out.dtype)


def owner_core(src_blk, src_dev, src_slot, src_live, my_slot, qd_all, stats_all, k_loc, v_loc, spread):
    sources = src_blk.shape[0]
    tokens, width = k_loc.shape
    full = pl.BlockSpec((tokens, width), lambda s, a, e, b, c, d: (0, 0))
    grid_spec = pltpu.PrefetchScalarGridSpec(
        num_scalar_prefetch=5,
        grid=(sources,),
        in_specs=[
            pl.BlockSpec((BLK, 2 * width), lambda s, a, e, b, c, d: (a[s], 0)),
            pl.BlockSpec((1, stats_all.shape[1], BLK), lambda s, a, e, b, c, d: (e[s], 0, b[s])),
            full,
            full,
            pl.BlockSpec(spread.shape, lambda s, a, e, b, c, d: (0, 0)),
        ],
        out_specs=[full, full],
        scratch_shapes=[pltpu.VMEM((tokens, width), jnp.float32), pltpu.VMEM((tokens, width), jnp.float32)],
    )
    return pl.pallas_call(
        _owner_body,
        grid_spec=grid_spec,
        out_shape=[
            jax.ShapeDtypeStruct((tokens, width), jnp.bfloat16),
            jax.ShapeDtypeStruct((tokens, width), jnp.bfloat16),
        ],
        compiler_params=pltpu.CompilerParams(dimension_semantics=("arbitrary",)),
        cost_estimate=pl.CostEstimate(
            flops=sources * 8 * BLK * BLK * width,
            transcendentals=sources * BLK * BLK * (width // HD),
            bytes_accessed=sources * BLK * 2 * width * 2 + 2 * tokens * width * (2 + 8),
        ),
    )(src_blk, src_dev, src_slot, src_live, my_slot, qd_all, stats_all, k_loc, v_loc, spread)


def shards(
    queries,
    key_states,
    value_states,
    out_grad,
    memory,
    near_device,
    near_slot,
    near_count,
    writer_block,
):
    seq_devices = lax.axis_size("seq")
    batch_devices = lax.axis_size("batch")
    my_index = lax.axis_index("seq")
    tokens = queries.shape[1]
    row_width = queries.shape[2]
    local_blocks = tokens // BLK
    rows_dev = MEM // seq_devices
    block_scale = 1.0 / math.sqrt(BLK)
    value_blocks = value_states[0].reshape(local_blocks, BLK, row_width)

    kv_all = lax.all_gather(
        jnp.concatenate([key_states[0], value_states[0]], axis=-1), "seq", axis=0, tiled=True
    )

    value_sums = jnp.sum(value_blocks, axis=1, dtype=jnp.float32)
    all_sums = lax.all_to_all(
        jnp.broadcast_to(value_sums[None], (seq_devices, local_blocks, row_width)),
        "seq",
        split_axis=0,
        concat_axis=0,
        tiled=True,
    ).reshape(seq_devices * local_blocks, row_width)
    memory_keys = (memory + jnp.take(all_sums, writer_block, axis=0) * block_scale).astype(
        jnp.bfloat16
    )
    near_block = (near_device * local_blocks + near_slot).astype(jnp.int32)
    my_near = lax.dynamic_slice_in_dim(near_block, my_index * local_blocks, local_blocks, 0).reshape(-1)
    my_count = lax.dynamic_slice_in_dim(near_count, my_index * local_blocks, local_blocks, 0)
    qd_all = lax.all_gather(
        jnp.concatenate([queries[0], out_grad[0]], axis=-1), "seq", axis=0, tiled=True
    )
    attended_rows, query_rows_grad, term, stats = query_core(
        my_count, my_near, queries[0], out_grad[0], memory_keys, kv_all
    )
    stats_all = lax.all_to_all(
        jnp.broadcast_to(stats[None], (seq_devices,) + stats.shape),
        "seq",
        split_axis=0,
        concat_axis=0,
        tiled=True,
    )
    row_parts = lax.all_to_all(
        jnp.sum(term, axis=0).astype(jnp.bfloat16).reshape(seq_devices, rows_dev, row_width),
        "seq",
        split_axis=0,
        concat_axis=0,
        tiled=True,
    )
    row_grads = jnp.sum(row_parts.astype(jnp.float32), axis=0)
    near_width = near_device.shape[1]
    entries = local_blocks * near_width
    target = near_device.reshape(seq_devices, entries)
    source_slot = near_slot.reshape(seq_devices, entries)
    live = (
        jnp.arange(near_width)[None, None, :]
        < near_count.reshape(seq_devices, local_blocks)[:, :, None]
    ).reshape(seq_devices, entries)
    names_me = target == my_index
    entry_at = jnp.argmax(names_me, axis=1).astype(jnp.int32)
    src_slot = entry_at // near_width
    src_blk = (jnp.arange(seq_devices, dtype=jnp.int32) * local_blocks + src_slot).astype(jnp.int32)
    src_live = jnp.any(names_me & live, axis=1).astype(jnp.int32)
    my_slot = jnp.sum(jnp.where(names_me, source_slot, 0), axis=1).astype(jnp.int32)
    order = jnp.argsort(1 - src_live, stable=True).astype(jnp.int32)
    live_count = jnp.sum(src_live)
    position = jnp.arange(seq_devices, dtype=jnp.int32)
    pick = jnp.where(position < live_count, order, order[jnp.maximum(live_count - 1, 0)])
    live_in_order = (position < live_count).astype(jnp.int32)
    my_writers = (
        lax.dynamic_slice_in_dim(writer_block, my_index * rows_dev, rows_dev, 0)
        - my_index * local_blocks
    )
    writer_match = (my_writers[:, None] == jnp.arange(local_blocks)[None, :])[:, :, None]
    spread = jnp.sum(jnp.where(writer_match, row_grads[:, None, :], 0.0), axis=0) * block_scale
    all_rows = lax.all_to_all(
        jnp.broadcast_to(row_grads[None], (batch_devices, rows_dev, row_width)),
        "batch",
        split_axis=0,
        concat_axis=0,
        tiled=True,
    )
    memory_grad = jnp.sum(all_rows, axis=0)
    memory_grad, qd_all = lax.optimization_barrier((memory_grad, qd_all))
    dk_sum, dv_sum = owner_core(
        src_blk[pick], pick, src_slot[pick], live_in_order, my_slot[pick], qd_all, stats_all,
        key_states[0], value_states[0], spread,
    )
    attended = attended_rows.reshape(1, tokens, row_width)
    query_grad = query_rows_grad.reshape(1, tokens, row_width)
    key_grad = dk_sum.reshape(1, tokens, row_width)
    value_grad = dv_sum.reshape(1, tokens, row_width)
    return (attended, query_grad, key_grad, value_grad, memory_grad)


def solution(mesh):
    placed = (
        P("batch", "seq", None),
        P("batch", "seq", None),
        P("batch", "seq", None),
        P("batch", "seq", None),
        P(),
        P(),
        P(),
        P(),
        P(),
    )
    return jax.shard_map(
        shards,
        mesh=mesh,
        in_specs=placed,
        out_specs=(
            P("batch", "seq", None),
            P("batch", "seq", None),
            P("batch", "seq", None),
            P("batch", "seq", None),
            P("seq", None),
        ),
        check_vma=False,
    )
```

profile of v0, /device:TPU:98, one launch (start us, length us, event | category | flops | bytes accessed | tf_op | source)
XLA Modules:
  0.0 318.1 jit_solution(17471480094528194058)
XLA Ops:
  7.3 2.3 pad_maximum_fusion
  9.6 0.0 all-gather.5.cloned.1.call-start
  9.7 2.3 pad_maximum_fusion.1
  12.0 0.1 convert_reduce_fusion.1
  12.1 0.8 broadcast_in_dim.69
  12.9 7.2 %all-to-all-start = ((f32[32,2,1024]{2,1,0:T(2,128)}), f32[32,2,1024]{2,1,0:T(2,128)S(1)}, u32[]{:S(2)}, u32[]{:S(2)}) async-start(f32[32,2,1024]{2,1,0:T(2,128)} %broadcast_in_dim.69), calls=%async_computation | async-start | bytes 524288 | tf_op jit(solution)/shard_map/all_to_all | solution.py:220
  20.1 1.2 select_reduce_fusion.1
  21.2 0.1 constant_dynamic-slice_fusion
  21.3 0.1 copy.17
  21.4 0.7 reshape.79.nb_ref
  22.1 0.6 dynamic_slice.12.cnt_ref
  22.7 3.1 all-to-all-done
  25.8 0.2 reshape.80
  26.0 5.4 %gather_fusion = f32[1024,1024]{1,0:T(8,128)} fusion(f32[64,1024]{1,0:T(8,128)S(1)} %reshape.80, s32[1024]{0:T(1024)S(1)} %fusion.2), kind=kCustom, calls=%fused_computation | custom fusion | bytes 8392704 | tf_op jit(solution)/shard_map/jit(_take)/gather | solution.py:227
  31.4 5.6 %add_convert_fusion.mk_ref = bf16[1024,1024]{1,0:T(8,128)(2,1)} fusion(f32[1024,1024]{1,0:T(8,128)} %param.13, f32[1024,1024]{1,0:T(8,128)} %gather_fusion, pred[1024]{0:T(1024)(128)(4,1)S(1)} %compare_and_fusion), kind=kLoop, calls=%fused_computation.5 | loop fusion | flops 4194304 | bytes 10486784 | tf_op jit(solution)/shard_map/convert_element_type | solution.py:227
  37.0 86.6 %all-gather.3.cloned.1.call-done.rest_0_.rest_1_.rest_2_.rest_3_.rest_4_.rest_5_.rest_6_.rest_7_.rest_8_.rest_9_.rest_10_.rest_11_.rest_12_.rest_13_.rest_14_.rest_15_ = bf16[8192,2048]{1,0:T(8,128)(2,1)} async-done(((bf16[256,2048]{1,0:T(8,128)(2,1)}), bf16[8192,2048]{1,0:T(8,128)(2,1)}) %all-gather.3.cloned.1.call-update) | async-done | bytes 33554448 | tf_op jit(solution)/shard_map/all_gather | solution.py:215
  123.6 30.6 %shard_map.128 = (bf16[256,1024]{1,0:T(8,128)(2,1)}, bf16[256,1024]{1,0:T(8,128)(2,1)}, f32[2,1024,1024]{2,1,0:T(8,128)}, f32[24,256]{1,0:T(8,128)}) custom-call(s32[2]{0:T(128)} %dynamic_slice.12.cnt_ref, s32[16]{0:T(128)} %reshape.79.nb_ref, bf16[256,1024]{1,0:T(8,128)(2,1)} %bitcast.19, bf16[256,1024]{1,0:T(8,128)(2,1)} %bitcast.21, ...), custom_call_target="tpu_custom_call" | custom-call | flops 5905580032 | bytes 23068672 | tf_op jit(solution)/shard_map/pallas_call | solution.py:97
  154.2 6.2 %reduce_sum.75 = bf16[1024,1024]{1,0:T(8,128)(2,1)} reduce(f32[2,1024,1024]{2,1,0:T(8,128)} %get-tuple-element.19, f32[]{:T(128)} %constant.30.clone.1), dimensions={0}, to_apply=%region_8.9 | reduce | flops 1048576 | bytes 10485764 | tf_op jit(solution)/shard_map/reduce_sum | solution.py:247
  160.4 7.6 %all-to-all-start.1 = ((bf16[32,32,1024]{2,1,0:T(8,128)(2,1)}), bf16[32,32,1024]{2,1,0:T(8,128)(2,1)S(1)}, u32[]{:S(2)}, u32[]{:S(2)}) async-start(bf16[32,32,1024]{2,1,0:T(8,128)(2,1)} %bitcast.12), calls=%async_computation.1 | async-start | bytes 4194304 | tf_op jit(solution)/shard_map/all_to_all | solution.py:246
  168.0 0.1 copy.18
  168.2 0.1 reduce_or.14
  168.3 0.1 reduce_or.18
  168.4 0.7 convert_reduce_fusion.2
  169.8 0.1 eq.32
  169.9 1.6 sort.17
  171.5 0.6 dynamic_slice.14
  172.1 1.9 compare_select_fusion.1
  174.0 42.1 %all-to-all-done.1 = bf16[32,32,1024]{2,1,0:T(8,128)(2,1)S(1)} async-done(((bf16[32,32,1024]{2,1,0:T(8,128)(2,1)}), bf16[32,32,1024]{2,1,0:T(8,128)(2,1)S(1)}, u32[]{:S(2)}, u32[]{:S(2)}) %all-to-all-start.1) | async-done | bytes 2097184 | tf_op jit(solution)/shard_map/all_to_all | solution.py:246
  216.1 0.4 convert_reduce_fusion
  216.5 0.8 broadcast_in_dim.75
  217.3 4.3 %all-to-all-start.2 = ((f32[4,32,1024]{2,1,0:T(8,128)}), f32[4,32,1024]{2,1,0:T(8,128)S(1)}, u32[]{:S(2)}, u32[]{:S(2)}) async-start(f32[4,32,1024]{2,1,0:T(8,128)} %broadcast_in_dim.75), calls=%async_computation.2 | async-start | bytes 1048576 | tf_op jit(solution)/shard_map/all_to_all | solution.py:279
  221.6 0.6 iota_reduce_fusion
  222.3 1.2 gather_fusion.1
  223.5 1.3 gather_fusion.2
  224.8 0.1 reduce_sum.73
  224.9 0.1 reduce_sum.74
  225.0 1.3 gather_fusion.3
  226.3 5.1 %all-to-all-done.2 = f32[4,32,1024]{2,1,0:T(8,128)S(1)} async-done(((f32[4,32,1024]{2,1,0:T(8,128)}), f32[4,32,1024]{2,1,0:T(8,128)S(1)}, u32[]{:S(2)}, u32[]{:S(2)}) %all-to-all-start.2) | async-done | bytes 524320 | tf_op jit(solution)/shard_map/all_to_all | solution.py:279
  231.4 1.0 broadcast_in_dim.76
  232.3 7.0 %all-to-all-start.3 = ((f32[32,24,256]{2,1,0:T(8,128)}), f32[32,24,256]{2,1,0:T(8,128)S(1)}, u32[]{:S(2)}, u32[]{:S(2)}) async-start(f32[32,24,256]{2,1,0:T(8,128)} %broadcast_in_dim.76), calls=%async_computation.3 | async-start | bytes 1572864 | tf_op jit(solution)/shard_map/all_to_all | solution.py:239
  239.4 1.3 compare_convert_fusion.src_live
  240.6 0.8 dynamic-slice_subtract_fusion
  241.4 0.1 select_reduce_fusion
  241.5 0.6 broadcast_multiply_fusion.sp_ref
  242.1 0.7 reduce_sum.77
  242.8 27.1 %all-gather.5.cloned.1.call-done.qd_ref = bf16[8192,2048]{1,0:T(8,128)(2,1)} async-done(((bf16[256,2048]{1,0:T(8,128)(2,1)}), bf16[8192,2048]{1,0:T(8,128)(2,1)}) %all-gather.5.cloned.1.call-update) | async-done | bytes 33554448 | tf_op jit(solution)/shard_map/all_gather | solution.py:233
  269.9 0.9 copy-done.1
  270.8 40.5 %shard_map.129 = (bf16[256,1024]{1,0:T(8,128)(2,1)}, bf16[256,1024]{1,0:T(8,128)(2,1)}) custom-call(s32[32]{0:T(128)} %gather_fusion.1, s32[32]{0:T(128)} %get-tuple-element.28.src_dev, s32[32]{0:T(128)} %gather_fusion.2, s32[32]{0:T(128)} %compare_convert_fusion.src_live, s32[32]{0:T(128)} %gather_fusion.3, ...), custom_call_target="tpu_custom_call" | custom-call | flops 4294967296 | bytes 22020096 | tf_op jit(solution)/shard_map/pallas_call | solution.py:178
  (30 shorter events, 0.2 us)
Async XLA Ops:
  7.2 4.8 %copy-start = (bf16[1,256,1024]{2,1,0:T(8,128)(2,1)S(1)}, bf16[1,256,1024]{2,1,0:T(8,128)(2,1)}, u32[]{:S(2)}) copy-start(bf16[1,256,1024]{2,1,0:T(8,128)(2,1)} %param.11) | copy-start | bytes 1572868
  7.2 12.9 %copy-start.3 = (s32[1024]{0:T(1024)S(1)}, s32[1024]{0:T(1024)}, u32[]{:S(2)}) copy-start(s32[1024]{0:T(1024)} %param.17) | copy-start | bytes 12292
  7.2 12.9 %copy-start.6 = (s32[64,8]{0,1:T(8,128)S(1)}, s32[64,8]{0,1:T(8,128)}, u32[]{:S(2)}) copy-start(s32[64,8]{0,1:T(8,128)} %param.14) | copy-start | bytes 6148
  7.2 12.9 %copy-start.5 = (s32[64,8]{0,1:T(8,128)S(1)}, s32[64,8]{0,1:T(8,128)}, u32[]{:S(2)}) copy-start(s32[64,8]{0,1:T(8,128)} %param.15) | copy-start | bytes 6148
  7.2 14.9 %copy-start.8 = (s32[64]{0:T(128)S(1)}, s32[64]{0:T(128)}, u32[]{:S(2)}) copy-start(s32[64]{0:T(128)} %param.16) | copy-start | bytes 772
  7.2 116.4 %all-gather.3.cloned.1.call-start = ((), (), s32[]{:S(2)}) async-start(), calls=%async_computation.4 | async-start | bytes 34603008 | tf_op jit(solution)/shard_map/all_gather | solution.py:215
  9.6 260.2 %all-gather.5.cloned.1.call-start = ((), (), s32[]{:S(2)}) async-start(), calls=%async_computation.5 | async-start | bytes 34603008 | tf_op jit(solution)/shard_map/all_gather | solution.py:233
  12.9 12.9 %all-to-all-start = ((f32[32,2,1024]{2,1,0:T(2,128)}), f32[32,2,1024]{2,1,0:T(2,128)S(1)}, u32[]{:S(2)}, u32[]{:S(2)}) async-start(f32[32,2,1024]{2,1,0:T(2,128)} %broadcast_in_dim.69), calls=%async_computation | async-start | bytes 524288 | tf_op jit(solution)/shard_map/all_to_all | solution.py:220
  160.4 7.6 %copy-start.4 = (pred[64,8]{0,1:T(8,128)(4,1)S(1)}, pred[64,8]{0,1:T(8,128)(4,1)}, u32[]{:S(2)}) copy-start(pred[64,8]{0,1:T(8,128)(4,1)} %get-tuple-element.26) | copy-start | bytes 1540
  160.4 7.7 %copy-start.9 = (s32[64]{0:T(128)S(1)}, s32[64]{0:T(128)}, u32[]{:S(2)}) copy-start(s32[64]{0:T(128)} %param.16) | copy-start | bytes 772
  160.4 64.4 %copy-start.7 = (s32[64]{0:T(128)S(1)}, s32[64]{0:T(128)}, u32[]{:S(2)}) copy-start(s32[64]{0:T(128)} %get-tuple-element.25) | copy-start | bytes 772
  160.4 71.0 %copy-start.2 = (f32[24,256]{1,0:T(8,128)S(1)}, f32[24,256]{1,0:T(8,128)}, u32[]{:S(2)}) copy-start(f32[24,256]{1,0:T(8,128)} %get-tuple-element.21) | copy-start | bytes 73732
  160.4 55.7 %all-to-all-start.1 = ((bf16[32,32,1024]{2,1,0:T(8,128)(2,1)}), bf16[32,32,1024]{2,1,0:T(8,128)(2,1)S(1)}, u32[]{:S(2)}, u32[]{:S(2)}) async-start(bf16[32,32,1024]{2,1,0:T(8,128)(2,1)} %bitcast.12), calls=%async_computation.1 | async-start | bytes 4194304 | tf_op jit(solution)/shard_map/all_to_all | solution.py:246
  217.3 14.1 %all-to-all-start.2 = ((f32[4,32,1024]{2,1,0:T(8,128)}), f32[4,32,1024]{2,1,0:T(8,128)S(1)}, u32[]{:S(2)}, u32[]{:S(2)}) async-start(f32[4,32,1024]{2,1,0:T(8,128)} %broadcast_in_dim.75), calls=%async_computation.2 | async-start | bytes 1048576 | tf_op jit(solution)/shard_map/all_to_all | solution.py:279
  232.3 37.5 %all-to-all-start.3 = ((f32[32,24,256]{2,1,0:T(8,128)}), f32[32,24,256]{2,1,0:T(8,128)S(1)}, u32[]{:S(2)}, u32[]{:S(2)}) async-start(f32[32,24,256]{2,1,0:T(8,128)} %broadcast_in_dim.76), calls=%async_computation.3 | async-start | bytes 1572864 | tf_op jit(solution)/shard_map/all_to_all | solution.py:239
  269.9 0.9 copy-start.1
Sparse Core Ops, SparseCore 0:
  10.3 113.2 all-gather.2
  125.9 143.9 all-gather.4
where the time goes:
time: 317 us; the launch traced here: 318 us
  waiting for transfers between devices  164 us (52%)
  Pallas kernels  71.1 us (22%)
  other arithmetic  26.6 us (8%)
  starting transfers between devices  26.1 us (8%)
  local copies, waits for them, and re-layouts  15.4 us (5%)
  between operations  14.9 us (5%)
    all_gather x1, waiting for transfers between devices, shards(): lax.all_gather(jnp.concatenate([key_states[0], value_states[0]], axis=-1)...  86.6 us
    all_to_all x1, waiting for transfers between devices, shards(): lax.all_to_all(jnp.sum(term, axis=0).astype(jnp.bfloat16).reshape(seq_dev...  42.1 us
    pallas_call x1, Pallas kernels, owner_core(): pl.pallas_call(_owner_body, grid_spec=grid_spec, out_shape=[jax.ShapeDtyp...  40.5 us
    pallas_call x1, Pallas kernels, query_core(): pl.pallas_call(_query_body, grid_spec=grid_spec, out_shape=[jax.ShapeDtyp...  30.6 us
    all_gather x1, waiting for transfers between devices, shards(): lax.all_gather(jnp.concatenate([queries[0], out_grad[0]], axis=-1), 'seq'...  27.1 us
    all_to_all x1, starting transfers between devices, shards(): lax.all_to_all(jnp.sum(term, axis=0).astype(jnp.bfloat16).reshape(seq_dev...  7.6 us
    all_to_all x1, starting transfers between devices, shards(): lax.all_to_all(jnp.broadcast_to(value_sums[None], (seq_devices, local_blo...  7.16 us
    all_to_all x1, starting transfers between devices, shards(): lax.all_to_all(jnp.broadcast_to(stats[None], (seq_devices,) + stats.shape...  7 us
  transfers between devices with their start and end apart: 6, of which 5 were waited for; matrix products, arithmetic and copies ran while one was open for 12% of the time, Pallas kernels for 10%

commit v1 on v0

--- a/solution.py
+++ b/solution.py
@@ -141,7 +141,7 @@
             row_total = st[heads + h : heads + h + 1]
             grad_dot = st[2 * heads + h : 2 * heads + h + 1]
             score_t = lax.dot_general(k_h, q_h, nt, preferred_element_type=f32) * scale
-            prob_t = jnp.exp(score_t - row_max) / row_total
+            prob_t = jnp.exp(score_t - row_max) * (1.0 / row_total)
             weight_t = prob_t.astype(jnp.bfloat16)
             dprob_t = lax.dot_general(v_h, do_h, nt, preferred_element_type=f32)
             dscore_t = (prob_t * (dprob_t - grad_dot)).astype(jnp.bfloat16)

time: 317 us -> 318 us (level)
  the two profiles are of different devices: /device:TPU:98 before, /device:TPU:103 now
where the time goes in v1:
time: 318 us; the launch traced here: 315 us
  waiting for transfers between devices  165 us (52%)
  Pallas kernels  68 us (21%)
  other arithmetic  26.6 us (8%)
  starting transfers between devices  25.9 us (8%)
  local copies, waits for them, and re-layouts  15.4 us (5%)
  between operations  14.9 us (5%)
    all_gather x1, waiting for transfers between devices, shards(): lax.all_gather(jnp.concatenate([key_states[0], value_states[0]], axis=-1)...  85.5 us
    all_to_all x1, waiting for transfers between devices, shards(): lax.all_to_all(jnp.sum(term, axis=0).astype(jnp.bfloat16).reshape(seq_dev...  42.4 us
    pallas_call x1, Pallas kernels, owner_core(): pl.pallas_call(_owner_body, grid_spec=grid_spec, out_shape=[jax.ShapeDtyp...  37.5 us
    pallas_call x1, Pallas kernels, query_core(): pl.pallas_call(_query_body, grid_spec=grid_spec, out_shape=[jax.ShapeDtyp...  30.6 us
    all_gather x1, waiting for transfers between devices, shards(): lax.all_gather(jnp.concatenate([queries[0], out_grad[0]], axis=-1), 'seq'...  27.2 us
    all_to_all x1, starting transfers between devices, shards(): lax.all_to_all(jnp.sum(term, axis=0).astype(jnp.bfloat16).reshape(seq_dev...  7.49 us
    all_to_all x1, starting transfers between devices, shards(): lax.all_to_all(jnp.broadcast_to(value_sums[None], (seq_devices, local_blo...  7.41 us
    all_to_all x1, starting transfers between devices, shards(): lax.all_to_all(jnp.broadcast_to(stats[None], (seq_devices,) + stats.shape...  6.87 us
  transfers between devices with their start and end apart: 6, of which 5 were waited for; matrix products, arithmetic and copies ran while one was open for 12% of the time, Pallas kernels for 10%

profile of v1, /device:TPU:103, one launch (start us, length us, event | category | flops | bytes accessed | tf_op | source)
XLA Modules:
  0.0 315.5 jit_solution(15181841115707139457)
XLA Ops:
  7.3 2.3 pad_maximum_fusion
  9.6 0.0 all-gather.5.cloned.1.call-start
  9.7 2.3 pad_maximum_fusion.1
  12.0 0.1 convert_reduce_fusion.1
  12.1 0.8 broadcast_in_dim.69
  12.9 7.4 %all-to-all-start = ((f32[32,2,1024]{2,1,0:T(2,128)}), f32[32,2,1024]{2,1,0:T(2,128)S(1)}, u32[]{:S(2)}, u32[]{:S(2)}) async-start(f32[32,2,1024]{2,1,0:T(2,128)} %broadcast_in_dim.69), calls=%async_computation | async-start | bytes 524288 | tf_op jit(solution)/shard_map/all_to_all | solution.py:220
  20.3 1.2 select_reduce_fusion.1
  21.5 0.1 constant_dynamic-slice_fusion
  21.6 0.1 copy.17
  21.7 0.7 reshape.79.nb_ref
  22.3 0.6 dynamic_slice.12.cnt_ref
  23.0 4.4 %all-to-all-done = f32[32,2,1024]{2,1,0:T(2,128)S(1)} async-done(((f32[32,2,1024]{2,1,0:T(2,128)}), f32[32,2,1024]{2,1,0:T(2,128)S(1)}, u32[]{:S(2)}, u32[]{:S(2)}) %all-to-all-start) | async-done | bytes 262176 | tf_op jit(solution)/shard_map/all_to_all | solution.py:220
  27.3 0.2 reshape.80
  27.5 5.4 %gather_fusion = f32[1024,1024]{1,0:T(8,128)} fusion(f32[64,1024]{1,0:T(8,128)S(1)} %reshape.80, s32[1024]{0:T(1024)S(1)} %fusion.2), kind=kCustom, calls=%fused_computation | custom fusion | bytes 8392704 | tf_op jit(solution)/shard_map/jit(_take)/gather | solution.py:227
  32.9 5.6 %add_convert_fusion.mk_ref = bf16[1024,1024]{1,0:T(8,128)(2,1)} fusion(f32[1024,1024]{1,0:T(8,128)} %param.13, f32[1024,1024]{1,0:T(8,128)} %gather_fusion, pred[1024]{0:T(1024)(128)(4,1)S(1)} %compare_and_fusion), kind=kLoop, calls=%fused_computation.5 | loop fusion | flops 4194304 | bytes 10486784 | tf_op jit(solution)/shard_map/convert_element_type | solution.py:227
  38.5 85.5 %all-gather.3.cloned.1.call-done.rest_0_.rest_1_.rest_2_.rest_3_.rest_4_.rest_5_.rest_6_.rest_7_.rest_8_.rest_9_.rest_10_.rest_11_.rest_12_.rest_13_.rest_14_.rest_15_ = bf16[8192,2048]{1,0:T(8,128)(2,1)} async-done(((bf16[256,2048]{1,0:T(8,128)(2,1)}), bf16[8192,2048]{1,0:T(8,128)(2,1)}) %all-gather.3.cloned.1.call-update) | async-done | bytes 33554448 | tf_op jit(solution)/shard_map/all_gather | solution.py:215
  124.0 30.6 %shard_map.128 = (bf16[256,1024]{1,0:T(8,128)(2,1)}, bf16[256,1024]{1,0:T(8,128)(2,1)}, f32[2,1024,1024]{2,1,0:T(8,128)}, f32[24,256]{1,0:T(8,128)}) custom-call(s32[2]{0:T(128)} %dynamic_slice.12.cnt_ref, s32[16]{0:T(128)} %reshape.79.nb_ref, bf16[256,1024]{1,0:T(8,128)(2,1)} %bitcast.19, bf16[256,1024]{1,0:T(8,128)(2,1)} %bitcast.21, ...), custom_call_target="tpu_custom_call" | custom-call | flops 5905580032 | bytes 23068672 | tf_op jit(solution)/shard_map/pallas_call | solution.py:97
  154.6 6.2 %reduce_sum.75 = bf16[1024,1024]{1,0:T(8,128)(2,1)} reduce(f32[2,1024,1024]{2,1,0:T(8,128)} %get-tuple-element.19, f32[]{:T(128)} %constant.30.clone.1), dimensions={0}, to_apply=%region_8.9 | reduce | flops 1048576 | bytes 10485764 | tf_op jit(solution)/shard_map/reduce_sum | solution.py:247
  160.8 7.5 %all-to-all-start.1 = ((bf16[32,32,1024]{2,1,0:T(8,128)(2,1)}), bf16[32,32,1024]{2,1,0:T(8,128)(2,1)S(1)}, u32[]{:S(2)}, u32[]{:S(2)}) async-start(bf16[32,32,1024]{2,1,0:T(8,128)(2,1)} %bitcast.12), calls=%async_computation.1 | async-start | bytes 4194304 | tf_op jit(solution)/shard_map/all_to_all | solution.py:246
  168.3 0.1 copy.18
  168.4 0.1 reduce_or.14
  168.6 0.1 reduce_or.18
  168.7 0.7 convert_reduce_fusion.2
  170.1 0.1 eq.32
  170.2 1.6 sort.17
  171.8 0.6 dynamic_slice.14
  172.4 1.9 compare_select_fusion.1
  174.2 42.4 %all-to-all-done.1 = bf16[32,32,1024]{2,1,0:T(8,128)(2,1)S(1)} async-done(((bf16[32,32,1024]{2,1,0:T(8,128)(2,1)}), bf16[32,32,1024]{2,1,0:T(8,128)(2,1)S(1)}, u32[]{:S(2)}, u32[]{:S(2)}) %all-to-all-start.1) | async-done | bytes 2097184 | tf_op jit(solution)/shard_map/all_to_all | solution.py:246
  216.6 0.4 convert_reduce_fusion
  217.0 0.8 broadcast_in_dim.75
  217.9 4.0 %all-to-all-start.2 = ((f32[4,32,1024]{2,1,0:T(8,128)}), f32[4,32,1024]{2,1,0:T(8,128)S(1)}, u32[]{:S(2)}, u32[]{:S(2)}) async-start(f32[4,32,1024]{2,1,0:T(8,128)} %broadcast_in_dim.75), calls=%async_computation.2 | async-start | bytes 1048576 | tf_op jit(solution)/shard_map/all_to_all | solution.py:279
  221.9 0.6 iota_reduce_fusion
  222.5 1.2 gather_fusion.1
  223.7 1.3 gather_fusion.2
  225.0 0.1 reduce_sum.73
  225.1 0.1 reduce_sum.74
  225.2 1.3 gather_fusion.3
  226.5 5.2 %all-to-all-done.2 = f32[4,32,1024]{2,1,0:T(8,128)S(1)} async-done(((f32[4,32,1024]{2,1,0:T(8,128)}), f32[4,32,1024]{2,1,0:T(8,128)S(1)}, u32[]{:S(2)}, u32[]{:S(2)}) %all-to-all-start.2) | async-done | bytes 524320 | tf_op jit(solution)/shard_map/all_to_all | solution.py:279
  231.8 1.0 broadcast_in_dim.76
  232.7 6.9 %all-to-all-start.3 = ((f32[32,24,256]{2,1,0:T(8,128)}), f32[32,24,256]{2,1,0:T(8,128)S(1)}, u32[]{:S(2)}, u32[]{:S(2)}) async-start(f32[32,24,256]{2,1,0:T(8,128)} %broadcast_in_dim.76), calls=%async_computation.3 | async-start | bytes 1572864 | tf_op jit(solution)/shard_map/all_to_all | solution.py:239
  239.6 1.3 compare_convert_fusion.src_live
  240.9 0.8 dynamic-slice_subtract_fusion
  241.6 0.1 select_reduce_fusion
  241.8 0.6 broadcast_multiply_fusion.sp_ref
  242.4 0.7 reduce_sum.77
  243.0 27.2 %all-gather.5.cloned.1.call-done.qd_ref = bf16[8192,2048]{1,0:T(8,128)(2,1)} async-done(((bf16[256,2048]{1,0:T(8,128)(2,1)}), bf16[8192,2048]{1,0:T(8,128)(2,1)}) %all-gather.5.cloned.1.call-update) | async-done | bytes 33554448 | tf_op jit(solution)/shard_map/all_gather | solution.py:233
  270.2 0.9 copy-done.1
  271.1 37.5 %shard_map.129 = (bf16[256,1024]{1,0:T(8,128)(2,1)}, bf16[256,1024]{1,0:T(8,128)(2,1)}) custom-call(s32[32]{0:T(128)} %gather_fusion.1, s32[32]{0:T(128)} %get-tuple-element.28.src_dev, s32[32]{0:T(128)} %gather_fusion.2, s32[32]{0:T(128)} %compare_convert_fusion.src_live, s32[32]{0:T(128)} %gather_fusion.3, ...), custom_call_target="tpu_custom_call" | custom-call | flops 4294967296 | bytes 22020096 | tf_op jit(solution)/shard_map/pallas_call | solution.py:178
  (30 shorter events, 0.2 us)
Async XLA Ops:
  7.2 4.8 %copy-start = (bf16[1,256,1024]{2,1,0:T(8,128)(2,1)S(1)}, bf16[1,256,1024]{2,1,0:T(8,128)(2,1)}, u32[]{:S(2)}) copy-start(bf16[1,256,1024]{2,1,0:T(8,128)(2,1)} %param.11) | copy-start | bytes 1572868
  7.2 13.1 %copy-start.3 = (s32[1024]{0:T(1024)S(1)}, s32[1024]{0:T(1024)}, u32[]{:S(2)}) copy-start(s32[1024]{0:T(1024)} %param.17) | copy-start | bytes 12292
  7.2 13.1 %copy-start.6 = (s32[64,8]{0,1:T(8,128)S(1)}, s32[64,8]{0,1:T(8,128)}, u32[]{:S(2)}) copy-start(s32[64,8]{0,1:T(8,128)} %param.14) | copy-start | bytes 6148
  7.2 13.1 %copy-start.5 = (s32[64,8]{0,1:T(8,128)S(1)}, s32[64,8]{0,1:T(8,128)}, u32[]{:S(2)}) copy-start(s32[64,8]{0,1:T(8,128)} %param.15) | copy-start | bytes 6148
  7.2 15.1 %copy-start.8 = (s32[64]{0:T(128)S(1)}, s32[64]{0:T(128)}, u32[]{:S(2)}) copy-start(s32[64]{0:T(128)} %param.16) | copy-start | bytes 772
  7.2 116.8 %all-gather.3.cloned.1.call-start = ((), (), s32[]{:S(2)}) async-start(), calls=%async_computation.4 | async-start | bytes 34603008 | tf_op jit(solution)/shard_map/all_gather | solution.py:215
  9.6 260.6 %all-gather.5.cloned.1.call-start = ((), (), s32[]{:S(2)}) async-start(), calls=%async_computation.5 | async-start | bytes 34603008 | tf_op jit(solution)/shard_map/all_gather | solution.py:233
  12.9 14.5 %all-to-all-start = ((f32[32,2,1024]{2,1,0:T(2,128)}), f32[32,2,1024]{2,1,0:T(2,128)S(1)}, u32[]{:S(2)}, u32[]{:S(2)}) async-start(f32[32,2,1024]{2,1,0:T(2,128)} %broadcast_in_dim.69), calls=%async_computation | async-start | bytes 524288 | tf_op jit(solution)/shard_map/all_to_all | solution.py:220
  160.8 7.5 %copy-start.4 = (pred[64,8]{0,1:T(8,128)(4,1)S(1)}, pred[64,8]{0,1:T(8,128)(4,1)}, u32[]{:S(2)}) copy-start(pred[64,8]{0,1:T(8,128)(4,1)} %get-tuple-element.26) | copy-start | bytes 1540
  160.8 7.6 %copy-start.9 = (s32[64]{0:T(128)S(1)}, s32[64]{0:T(128)}, u32[]{:S(2)}) copy-start(s32[64]{0:T(128)} %param.16) | copy-start | bytes 772
  160.8 64.2 %copy-start.7 = (s32[64]{0:T(128)S(1)}, s32[64]{0:T(128)}, u32[]{:S(2)}) copy-start(s32[64]{0:T(128)} %get-tuple-element.25) | copy-start | bytes 772
  160.8 71.0 %copy-start.2 = (f32[24,256]{1,0:T(8,128)S(1)}, f32[24,256]{1,0:T(8,128)}, u32[]{:S(2)}) copy-start(f32[24,256]{1,0:T(8,128)} %get-tuple-element.21) | copy-start | bytes 73732
  160.8 55.9 %all-to-all-start.1 = ((bf16[32,32,1024]{2,1,0:T(8,128)(2,1)}), bf16[32,32,1024]{2,1,0:T(8,128)(2,1)S(1)}, u32[]{:S(2)}, u32[]{:S(2)}) async-start(bf16[32,32,1024]{2,1,0:T(8,128)(2,1)} %bitcast.12), calls=%async_computation.1 | async-start | bytes 4194304 | tf_op jit(solution)/shard_map/all_to_all | solution.py:246
  217.9 13.9 %all-to-all-start.2 = ((f32[4,32,1024]{2,1,0:T(8,128)}), f32[4,32,1024]{2,1,0:T(8,128)S(1)}, u32[]{:S(2)}, u32[]{:S(2)}) async-start(f32[4,32,1024]{2,1,0:T(8,128)} %broadcast_in_dim.75), calls=%async_computation.2 | async-start | bytes 1048576 | tf_op jit(solution)/shard_map/all_to_all | solution.py:279
  232.7 37.5 %all-to-all-start.3 = ((f32[32,24,256]{2,1,0:T(8,128)}), f32[32,24,256]{2,1,0:T(8,128)S(1)}, u32[]{:S(2)}, u32[]{:S(2)}) async-start(f32[32,24,256]{2,1,0:T(8,128)} %broadcast_in_dim.76), calls=%async_computation.3 | async-start | bytes 1572864 | tf_op jit(solution)/shard_map/all_to_all | solution.py:239
  270.2 0.9 copy-start.1
Sparse Core Ops, SparseCore 0:
  10.3 113.6 all-gather.2
  126.3 143.9 all-gather.4
